TPU v7x, 512 devices: a whole 4x4x16 slice. The times are simulated.
512 devices in a mesh: rx: 64 (over z_lo, x, core), band: 8 (over y, z_hi).
Axes of the slice: x: 4, y: 4, z: 16 (z_hi: 2, z_lo: 8; z = z_hi * 8 + z_lo), core: 2. Of those that a mesh axis runs over, the one named last changes fastest.
Arguments:
- spectra: bfloat16 [2, 256, 64, 8192], P(None, 'band', None, 'rx'), may hold values from -6 to 6
- source_index: int32 [64], replicated, may hold values from 0 to 8191, as said below
Outputs:
- stack: bfloat16 [2, 256, 64, 8192], P(None, 'band', None, 'rx')
Inputs may be any that keep to these rules, and one draw needn't show every extreme that they name: `source_index`: virtual source s is one of channels s * 128 to (s + 1) * 128 - 1; the first and the last channel are sources.
All inputs are finite; a program needn't handle non-finite values.
Results may differ from a plain program's by a relative error of at most 0.0059.
Values may be sent and summed in bfloat16 or wider, within the bound.
A program may use at most 64 MiB of HBM per device.

v0:
```python
import jax
import jax.numpy as jnp
from jax import lax
from jax.sharding import PartitionSpec as P

HALF = 4


def padded_2(block, sides, width):
    for axis, dim in sides:
        count = lax.axis_size(axis)
        forward = [(i, i + 1) for i in range(count - 1)]
        backward = [(target, source) for source, target in forward]
        low = lax.ppermute(
            lax.slice_in_dim(block, block.shape[dim] - width, None, axis=dim), axis, forward
        )
        high = lax.ppermute(lax.slice_in_dim(block, 0, width, axis=dim), axis, backward)
        block = jnp.concatenate([low, block, high], axis=dim)
    return block


def magnitude(values_in):
    values = values_in.astype(jnp.float32)
    rounded = lax.optimization_barrier(
        jnp.sqrt(values[0] * values[0] + values[1] * values[1]).astype(jnp.bfloat16)
    )
    return rounded


def whiten(spectra):
    bin_count = spectra.shape[1]
    padded = padded_2(spectra, (("band", 1),), HALF)
    amplitude = magnitude(padded).astype(jnp.float32)
    total = amplitude[0:bin_count]
    for offset in range(1, 2 * HALF + 1):
        total = total + amplitude[offset : offset + bin_count]
    smooth = total / (2 * HALF + 1)
    return (spectra.astype(jnp.float32) / (smooth + 0.1)[None]).astype(jnp.bfloat16)


def cross_spectra(whitened, source_rows):
    bin_count = whitened.shape[1]
    window_count = whitened.shape[2]
    sources = source_rows.reshape(source_rows.shape[0], 2, bin_count, window_count)
    source_real = sources[:, 0]
    source_imag = sources[:, 1]
    coefficients = jnp.stack(
        [jnp.stack([source_real, source_imag], 0), jnp.stack([-source_imag, source_real], 0)], 0
    )
    products = jnp.einsum(
        "oqnfw,qfwc->ofnc", coefficients, whitened, preferred_element_type=jnp.float32
    )
    return (products / window_count).astype(jnp.bfloat16)


def local(spectra, source_index):
    whitened = whiten(spectra)
    device_rank = lax.axis_index("rx")
    channels_here = spectra.shape[3]
    local_column = source_index[device_rank] - device_rank * channels_here
    own_row = lax.dynamic_slice_in_dim(whitened, local_column, 1, 3).reshape(1, -1)
    collected = lax.all_gather(own_row, "rx", axis=0, tiled=True)
    return cross_spectra(whitened, collected)


def solution(mesh):
    return jax.shard_map(
        local,
        mesh=mesh,
        in_specs=(P(None, "band", None, "rx"), P()),
        out_specs=P(None, "band", None, "rx"),
        check_vma=False,
    )
```

profile of v0, /device:TPU:9, one launch (start us, length us, event | category | flops | bytes accessed | tf_op | source)
XLA Modules:
  0.0 175.7 jit_solution(2140125977759759294)
XLA Ops:
  0.0 1.0 fusion.20
  1.0 15.4 %collective-permute-start = (bf16[2,4,64,128]{3,2,1,0:T(8,128)(2,1)S(1)}, bf16[2,4,64,128]{3,2,1,0:T(8,128)(2,1)S(1)}, u32[]{:S(2)}, u32[]{:S(2)}) collective-permute-start(bf16[2,4,64,128]{3,2,1,0:T(8,128)(2,1)S(1)} %get-tuple-element.7), channel_id=1, source_target_pairs={{0,1},{1,2},{2,3},{3,4},{4,5},{5,6},{6,7},{8,9},{9,10},{10,11},{11... | collective-permute-start | bytes 393224 | tf_op jit(solution)/shard_map/ppermute | solution.py:14
  16.4 1.9 %collective-permute-start.1 = (bf16[2,4,64,128]{3,2,1,0:T(8,128)(2,1)S(1)}, bf16[2,4,64,128]{3,2,1,0:T(8,128)(2,1)S(1)}, u32[]{:S(2)}, u32[]{:S(2)}) collective-permute-start(bf16[2,4,64,128]{3,2,1,0:T(8,128)(2,1)S(1)} %get-tuple-element.8), channel_id=1, source_target_pairs={{1,0},{2,1},{3,2},{4,3},{5,4},{6,5},{7,6},{9,8},{10,9},{11,10},{12... | collective-permute-start | bytes 393224 | tf_op jit(solution)/shard_map/ppermute | solution.py:17
  18.4 1.2 dynamic_slice.6
  20.3 0.0 collective-permute-done
  20.3 20.6 %collective-permute-done.1 = bf16[2,4,64,128]{3,2,1,0:T(8,128)(2,1)S(1)} collective-permute-done((bf16[2,4,64,128]{3,2,1,0:T(8,128)(2,1)S(1)}, bf16[2,4,64,128]{3,2,1,0:T(8,128)(2,1)S(1)}, u32[]{:S(2)}, u32[]{:S(2)}) %collective-permute-start.1) | collective-permute-done | bytes 131104 | tf_op jit(solution)/shard_map/ppermute | solution.py:17
  40.9 1.4 maximum_convert_fusion
  42.3 0.5 fusion.16
  42.8 0.1 convert_element_type.28
  42.9 0.0 copy-start
  43.0 0.3 fusion.14
  43.3 0.9 copy-done
  44.2 0.3 divide_convert_fusion
  44.5 0.9 dynamic-slice_reduce_fusion
  45.5 0.1 reshape.24
  45.6 121.0 %all-gather = bf16[64,1,4096]{2,1,0:T(2,128)(2,1)S(1)} all-gather(bf16[1,1,4096]{2,1,0:T(2,128)(2,1)S(1)} %reshape.24), channel_id=1, replica_groups=mesh['rx'=64,'band'=8] {'rx'}, dimensions={0}, use_global_device_ids=true | all-gather | bytes 532480 | tf_op jit(solution)/shard_map/all_gather | solution.py:62
  166.5 3.9 %reduce.1 = bf16[64,4096]{1,0:T(8,128)(2,1)} reduce(bf16[64,1,4096]{2,1,0:T(2,128)(2,1)S(1)} %all-gather, bf16[]{:T(256)} %constant.20), dimensions={1}, to_apply=%all-gather.reduce_sub_computation | reduce | bytes 1048578 | tf_op jit(solution)/shard_map/all_gather | solution.py:62
  170.5 2.1 %reshape.23 = bf16[64,2,32,64]{3,2,1,0:T(8,128)(2,1)S(1)} reshape(bf16[64,4096]{1,0:T(8,128)(2,1)} %reduce.1) | data formatting | bytes 1048576 | tf_op jit(solution)/shard_map/reshape | solution.py:44
  172.5 0.1 fusion.19
  172.6 0.2 fusion.18
  172.9 0.4 copy_bitcast_fusion
  173.3 0.4 maximum_bitcast_fusion
  173.7 1.0 fusion.7
  174.7 1.1 copy.15
Async XLA Ops:
  1.0 19.3 %collective-permute-start = (bf16[2,4,64,128]{3,2,1,0:T(8,128)(2,1)S(1)}, bf16[2,4,64,128]{3,2,1,0:T(8,128)(2,1)S(1)}, u32[]{:S(2)}, u32[]{:S(2)}) collective-permute-start(bf16[2,4,64,128]{3,2,1,0:T(8,128)(2,1)S(1)} %get-tuple-element.7), channel_id=1, source_target_pairs={{0,1},{1,2},{2,3},{3,4},{4,5},{5,6},{6,7},{8,9},{9,10},{10,11},{11... | collective-permute-start | bytes 393224 | tf_op jit(solution)/shard_map/ppermute | solution.py:14
  16.4 24.4 %collective-permute-start.1 = (bf16[2,4,64,128]{3,2,1,0:T(8,128)(2,1)S(1)}, bf16[2,4,64,128]{3,2,1,0:T(8,128)(2,1)S(1)}, u32[]{:S(2)}, u32[]{:S(2)}) collective-permute-start(bf16[2,4,64,128]{3,2,1,0:T(8,128)(2,1)S(1)} %get-tuple-element.8), channel_id=1, source_target_pairs={{1,0},{2,1},{3,2},{4,3},{5,4},{6,5},{7,6},{9,8},{10,9},{11,10},{12... | collective-permute-start | bytes 393224 | tf_op jit(solution)/shard_map/ppermute | solution.py:17
  42.9 1.2 copy-start
where the time goes:
time: 176 us
  blocking collectives  121 us (69%)
  waiting for transfers between devices  20.6 us (12%)
  starting transfers between devices  17.4 us (10%)
  local copies, waits for them, and re-layouts  7.71 us (4%)
  other arithmetic  7.3 us (4%)
    all_gather x1, blocking collectives, local(): collected = lax.all_gather(own_row, 'rx', axis=0, tiled=True)  121 us
    ppermute x1, waiting for transfers between devices, padded_2(): lax.ppermute(lax.slice_in_dim(block, 0, width, axis=dim), axis, backward)  20.6 us
    ppermute x1, starting transfers between devices, padded_2(): lax.ppermute(lax.slice_in_dim(block, block.shape[dim] - width, None, axis...  15.4 us
    all_gather x1, other arithmetic, local(): collected = lax.all_gather(own_row, 'rx', axis=0, tiled=True)  3.94 us
  transfers between devices with their start and end apart: 2, of which 1 were waited for; matrix products, arithmetic and copies ran while one was open for 1% of the time, Pallas kernels for 0%

commit v1 on v0

--- a/solution.py
+++ b/solution.py
@@ -4,6 +4,11 @@
 from jax.sharding import PartitionSpec as P
 
 HALF = 4
+
+
+def all_by_exchange(x, axis, along):
+    repeated = jnp.stack([x] * lax.axis_size(axis))
+    return jnp.concatenate(lax.all_to_all(repeated, axis, 0, 0), axis=along)
 
 
 def padded_2(block, sides, width):
@@ -59,7 +64,7 @@
     channels_here = spectra.shape[3]
     local_column = source_index[device_rank] - device_rank * channels_here
     own_row = lax.dynamic_slice_in_dim(whitened, local_column, 1, 3).reshape(1, -1)
-    collected = lax.all_gather(own_row, "rx", axis=0, tiled=True)
+    collected = all_by_exchange(own_row, "rx", 0)
     return cross_spectra(whitened, collected)
 
 

time: 176 us -> 108 us (0.61)
  the two profiles are of different devices: /device:TPU:9 before, /device:TPU:1 now
where the time goes in v1:
time: 108 us; the launch traced here: 107 us
  blocking collectives  45.4 us (42%)
  starting transfers between devices  17.6 us (16%)
  waiting for transfers between devices  16.2 us (15%)
  local copies, waits for them, and re-layouts  14.4 us (13%)
  other arithmetic  11.9 us (11%)
    all_to_all x1, blocking collectives, all_by_exchange(): return jnp.concatenate(lax.all_to_all(repeated, axis, 0, 0), axis=along)  45.4 us
    ppermute x1, starting transfers between devices, padded_2(): lax.ppermute(lax.slice_in_dim(block, block.shape[dim] - width, None, axis...  16.3 us
    ppermute x1, waiting for transfers between devices, padded_2(): lax.ppermute(lax.slice_in_dim(block, 0, width, axis=dim), axis, backward)  16.2 us
    unnamed x4, local copies, waits for them, and re-layouts  5.92 us
    another operation x1, other arithmetic, all_by_exchange(): repeated = jnp.stack([x] * lax.axis_size(axis))  4.63 us
    all_to_all x1, other arithmetic, all_by_exchange(): return jnp.concatenate(lax.all_to_all(repeated, axis, 0, 0), axis=along)  3.94 us
  transfers between devices with their start and end apart: 2, of which 1 were waited for; matrix products, arithmetic and copies ran while one was open for 1% of the time, Pallas kernels for 0%

profile of v1, /device:TPU:1, one launch (start us, length us, event | category | flops | bytes accessed | tf_op | source)
XLA Modules:
  0.0 107.2 jit_solution(6092569536307160197)
XLA Ops:
  0.0 1.0 fusion.20
  1.0 16.3 %collective-permute-start = (bf16[2,4,64,128]{3,2,1,0:T(8,128)(2,1)S(1)}, bf16[2,4,64,128]{3,2,1,0:T(8,128)(2,1)S(1)}, u32[]{:S(2)}, u32[]{:S(2)}) collective-permute-start(bf16[2,4,64,128]{3,2,1,0:T(8,128)(2,1)S(1)} %get-tuple-element.7), channel_id=1, source_target_pairs={{0,1},{1,2},{2,3},{3,4},{4,5},{5,6},{6,7},{8,9},{9,10},{10,11},{11... | collective-permute-start | bytes 393224 | tf_op jit(solution)/shard_map/ppermute | solution.py:19
  17.3 1.3 %collective-permute-start.1 = (bf16[2,4,64,128]{3,2,1,0:T(8,128)(2,1)S(1)}, bf16[2,4,64,128]{3,2,1,0:T(8,128)(2,1)S(1)}, u32[]{:S(2)}, u32[]{:S(2)}) collective-permute-start(bf16[2,4,64,128]{3,2,1,0:T(8,128)(2,1)S(1)} %get-tuple-element.8), channel_id=1, source_target_pairs={{1,0},{2,1},{3,2},{4,3},{5,4},{6,5},{7,6},{9,8},{10,9},{11,10},{12... | collective-permute-start | bytes 393224 | tf_op jit(solution)/shard_map/ppermute | solution.py:22
  18.6 1.2 %dynamic_slice.6 = s32[1]{0:T(128)} dynamic-slice(s32[64]{0:T(128)} %param.3, s32[]{:T(128)S(6)} %select_n.6), dynamic_slice_sizes={1} | dynamic-slice | bytes 12 | tf_op jit(solution)/shard_map/dynamic_slice | solution.py:65
  20.5 0.0 collective-permute-done
  20.5 16.2 %collective-permute-done.1 = bf16[2,4,64,128]{3,2,1,0:T(8,128)(2,1)S(1)} collective-permute-done((bf16[2,4,64,128]{3,2,1,0:T(8,128)(2,1)S(1)}, bf16[2,4,64,128]{3,2,1,0:T(8,128)(2,1)S(1)}, u32[]{:S(2)}, u32[]{:S(2)}) %collective-permute-start.1) | collective-permute-done | bytes 131104 | tf_op jit(solution)/shard_map/ppermute | solution.py:22
  36.7 1.4 %maximum_convert_fusion = f32[2,40,64,128]{3,2,1,0:T(8,128)S(1)} fusion(bf16[2,4,64,128]{3,2,1,0:T(8,128)(2,1)S(1)} %collective-permute-done.1, bf16[2,32,64,128]{3,2,1,0:T(8,128)(2,1)} %param.2, bf16[2,4,64,128]{3,2,1,0:T(8,128)(2,1)S(1)} %collective-permute-done), kind=kLoop, calls=%fused_computation.13 | loop fusion | flops 1966080 | bytes 3932160 | tf_op jit(solution)/shard_map/convert_element_type | solution.py:28
  38.1 0.5 fusion.16
  38.6 0.1 convert_element_type.28
  38.7 0.0 copy-start
  38.7 0.3 fusion.14
  39.1 0.9 copy-done
  40.0 0.3 divide_convert_fusion
  40.3 0.9 dynamic-slice_reduce_fusion
  41.2 0.1 stack_reshape.2
  41.3 1.0 stack.19
  42.4 0.6 broadcast.9
  43.0 4.6 %reduce.3 = bf16[64,4096]{1,0:T(8,128)(2,1)} reduce(bf16[64,1,4096]{2,1,0:T(2,128)(2,1)S(1)} %stack.19, bf16[]{:T(256)} %broadcast.9), dimensions={1}, to_apply=%stack.19.reduce_sub_computation | reduce | bytes 1048578 | tf_op jit(solution)/shard_map/stack | solution.py:10
  47.6 1.4 %reshape.24 = bf16[64,2,2048]{2,1,0:T(2,128)(2,1)S(1)} reshape(bf16[64,4096]{1,0:T(8,128)(2,1)} %reduce.3) | data formatting | bytes 1048576
  49.0 45.4 %all_to_all.5 = bf16[64,2,2048]{2,1,0:T(2,128)(2,1)} all-to-all(bf16[64,2,2048]{2,1,0:T(2,128)(2,1)S(1)} %reshape.24), channel_id=1, replica_groups=mesh['rx'=64,'band'=8] {'rx'}, dimensions={0} | all-to-all | bytes 1048576 | tf_op jit(solution)/shard_map/all_to_all | solution.py:11
  94.4 3.6 %reshape.25 = bf16[64,1,4096]{2,1,0:T(2,128)(2,1)S(1)} reshape(bf16[64,2,2048]{2,1,0:T(2,128)(2,1)} %all_to_all.5) | data formatting | bytes 1048576
  98.0 3.9 %reduce.1 = bf16[64,4096]{1,0:T(8,128)(2,1)} reduce(bf16[64,1,4096]{2,1,0:T(2,128)(2,1)S(1)} %reshape.25, bf16[]{:T(256)} %constant.20), dimensions={1}, to_apply=%all_to_all.3.reduce_sub_computation | reduce | bytes 1048578 | tf_op jit(solution)/shard_map/all_to_all | solution.py:11
  102.0 2.1 %reshape_reshape.3 = bf16[64,2,32,64]{3,2,1,0:T(8,128)(2,1)S(1)} reshape(bf16[64,4096]{1,0:T(8,128)(2,1)} %reduce.1) | data formatting | bytes 1048576 | tf_op jit(solution)/shard_map/reshape;reshape | solution.py:49
  104.0 0.1 fusion.19
  104.1 0.2 fusion.18
  104.3 0.4 copy_bitcast_fusion
  104.8 0.4 maximum_bitcast_fusion
  105.2 1.0 fusion.7
  106.2 1.1 copy.15
Async XLA Ops:
  1.0 19.5 %collective-permute-start = (bf16[2,4,64,128]{3,2,1,0:T(8,128)(2,1)S(1)}, bf16[2,4,64,128]{3,2,1,0:T(8,128)(2,1)S(1)}, u32[]{:S(2)}, u32[]{:S(2)}) collective-permute-start(bf16[2,4,64,128]{3,2,1,0:T(8,128)(2,1)S(1)} %get-tuple-element.7), channel_id=1, source_target_pairs={{0,1},{1,2},{2,3},{3,4},{4,5},{5,6},{6,7},{8,9},{9,10},{10,11},{11... | collective-permute-start | bytes 393224 | tf_op jit(solution)/shard_map/ppermute | solution.py:19
  17.3 19.4 %collective-permute-start.1 = (bf16[2,4,64,128]{3,2,1,0:T(8,128)(2,1)S(1)}, bf16[2,4,64,128]{3,2,1,0:T(8,128)(2,1)S(1)}, u32[]{:S(2)}, u32[]{:S(2)}) collective-permute-start(bf16[2,4,64,128]{3,2,1,0:T(8,128)(2,1)S(1)} %get-tuple-element.8), channel_id=1, source_target_pairs={{1,0},{2,1},{3,2},{4,3},{5,4},{6,5},{7,6},{9,8},{10,9},{11,10},{12... | collective-permute-start | bytes 393224 | tf_op jit(solution)/shard_map/ppermute | solution.py:22
  38.7 1.2 %copy-start = (bf16[2,32,64,128]{3,2,1,0:T(8,128)(2,1)S(1)}, bf16[2,32,64,128]{3,2,1,0:T(8,128)(2,1)}, u32[]{:S(2)}) copy-start(bf16[2,32,64,128]{3,2,1,0:T(8,128)(2,1)} %param.2) | copy-start | bytes 3145732
